TPU v7x, 256 devices: a whole 4x4x8 slice. The times are simulated.
256 devices in a mesh: seq: 32 (over z, y), tp: 8 (over x, core).
Axes of the slice: x: 4, y: 4, z: 8, core: 2. Of those that a mesh axis runs over, the one named last changes fastest.
Arguments:
- tokens: bfloat16 [16384, 4096], P('seq'), may hold values from -80 to 80
- norm_gain: float32 [4096], replicated, may hold values from 0.1 to 1.9
- query_weight: bfloat16 [4096, 4096], P(None, 'tp'), may hold values from -1 to 1
- key_weight: bfloat16 [4096, 1024], P(None, 'tp'), may hold values from -8 to 8
- value_weight: bfloat16 [4096, 1024], P(None, 'tp'), may hold values from -0.09375 to 0.09375
- out_weight: bfloat16 [4096, 4096], P(None, 'tp'), may hold values from -1 to 1
- segments: int32 [16384], replicated, may hold values from 0 to 2, never falling along the last dimension, each value on 1 to 8192 neighbouring positions
Outputs:
- attn_out: bfloat16 [16384, 4096], P('seq', 'tp')
All inputs are finite; a program needn't handle non-finite values.
Results may differ from a plain program's by a relative error of at most 0.013.
The roundings to bfloat16 on the way count: a program that leaves them out, or rounds other values in their place, can miss the bound.
Values may be sent and summed in bfloat16 or wider, within the bound.
A program may use at most 128 MiB of HBM per device.

v0:
```python
import math
import jax
import jax.numpy as jnp
from jax import lax
from jax.sharding import PartitionSpec as P

HEAD_DIM = 128
WINDOW = 4096


def shifted(value, axis, steps):
    count = lax.axis_size(axis)
    leading, last = (max(0, -steps), min(count, count - steps))
    return lax.ppermute(value, axis, [(source, source + steps) for source in range(leading, last)])


def rotate(vectors, positions):
    half_dim = vectors.shape[-1] // 2
    freqs = 10000.0 ** (-(jnp.arange(half_dim, dtype=jnp.float32) * 2.0 / vectors.shape[-1]))
    angles = positions[:, None] * freqs[None, :]
    cosine = jnp.cos(angles)[:, None, :]
    sine_part = jnp.sin(angles)[:, None, :]
    first = vectors[..., :half_dim]
    second = vectors[..., half_dim:]
    return jnp.concatenate(
        [first * cosine - second * sine_part, second * cosine + first * sine_part], axis=-1
    )


def project(normed, weight, positions):
    product = jnp.dot(normed, weight, preferred_element_type=jnp.float32)
    shaped = product.reshape(product.shape[0], -1, HEAD_DIM)
    return rotate(shaped, positions).astype(jnp.bfloat16)


def attend(queries, keys, values, allowed):
    block_rows, query_heads, head_size = queries.shape
    value_heads = keys.shape[1]
    grouped = queries.reshape(block_rows, value_heads, query_heads // value_heads, head_size)
    scores = jnp.einsum(
        "tkgd,skd->kgts", grouped, keys, preferred_element_type=jnp.float32
    ) / math.sqrt(head_size)
    scores = jnp.where(allowed[None, None], scores, jnp.float32(-1e30))
    peak = jnp.max(scores, axis=-1, keepdims=True)
    weights = jnp.exp(scores - peak)
    totals = jnp.sum(weights, axis=-1, keepdims=True)
    probabilities = (weights / totals).astype(jnp.bfloat16)
    attended = jnp.einsum(
        "kgts,skd->tkgd", probabilities, values, preferred_element_type=jnp.float32
    )
    return attended.reshape(block_rows, query_heads * head_size).astype(jnp.bfloat16)


def shards(tokens, norm_gain, query_weight, key_weight, value_weight, out_weight, segments):
    block_rows = tokens.shape[0]
    seq_index = lax.axis_index("seq")
    seq_count = lax.axis_size("seq")
    halo_blocks = min((WINDOW + block_rows - 2) // block_rows, seq_count - 1)
    widened = tokens.astype(jnp.float32)
    scale = lax.rsqrt(jnp.mean(widened * widened, axis=-1, keepdims=True) + 1e-05)
    normed = (widened * scale * norm_gain[None, :]).astype(jnp.bfloat16)
    first_token = seq_index * block_rows
    positions = (first_token + jnp.arange(block_rows, dtype=jnp.int32)).astype(jnp.float32)
    queries = project(normed, query_weight, positions)
    keys = project(normed, key_weight, positions)
    value_heads = keys.shape[1]
    values = jnp.dot(normed, value_weight, preferred_element_type=jnp.float32).astype(jnp.bfloat16)
    key_width = value_heads * HEAD_DIM
    key_value = jnp.concatenate([keys.reshape(block_rows, key_width), values], axis=1)
    front = halo_blocks * block_rows
    known_blocks = key_value
    gathered_count = 0
    while gathered_count < halo_blocks:
        taking = min(gathered_count + 1, halo_blocks - gathered_count)
        outgoing = known_blocks[known_blocks.shape[0] - taking * block_rows :]
        incoming = shifted(outgoing, "seq", gathered_count + 1)
        known_blocks = jnp.concatenate([incoming, known_blocks], axis=0)
        gathered_count = gathered_count + taking
    before = known_blocks[:front]
    window_rows = jnp.concatenate([before, key_value], axis=0)
    span = window_rows.shape[0]
    window_keys = window_rows[:, :key_width].reshape(span, value_heads, HEAD_DIM)
    window_values = window_rows[:, key_width:].reshape(span, value_heads, HEAD_DIM)
    padded_segments = jnp.concatenate([jnp.full((front,), -1, jnp.int32), segments], axis=0)
    start_index = seq_index * block_rows
    key_segments = lax.dynamic_slice_in_dim(padded_segments, start_index, span, 0)
    query_segments = lax.dynamic_slice_in_dim(segments, start_index, block_rows, 0)
    query_pos = start_index + jnp.arange(block_rows, dtype=jnp.int32)
    key_pos = start_index - front + jnp.arange(span, dtype=jnp.int32)
    distance = query_pos[:, None] - key_pos[None, :]
    allowed = (
        (distance >= 0) & (distance < WINDOW) & (key_segments[None, :] == query_segments[:, None])
    )
    attended = attend(queries, window_keys, window_values, allowed)
    projected = jnp.dot(
        lax.all_gather(attended, "tp", axis=1, tiled=True),
        out_weight,
        preferred_element_type=jnp.float32,
    )
    return projected.astype(jnp.bfloat16)


def solution(mesh):
    return jax.shard_map(
        shards,
        mesh=mesh,
        in_specs=(
            P("seq", None),
            P(),
            P(None, "tp"),
            P(None, "tp"),
            P(None, "tp"),
            P(None, "tp"),
            P(),
        ),
        out_specs=P("seq", "tp"),
        check_vma=False,
    )
```

profile of v0, /device:TPU:1, one launch (start us, length us, event | category | flops | bytes accessed | tf_op | source)
XLA Modules:
  0.0 180.7 jit_solution(8147630564713881535)
XLA Ops:
  6.5 0.0 copy-start
  6.5 0.0 copy-start.15
  6.5 0.0 all-gather.2.cloned.1.call-start
  6.6 0.0 copy-start.2
  6.6 3.2 %fusion.6 = f32[512]{0:T(512)S(1)} fusion(bf16[512,4096]{1,0:T(8,128)(2,1)} %param.7), kind=kLoop, calls=%fused_computation.13 | loop fusion | flops 6290944 | bytes 4196352 | tf_op jit(solution)/shard_map/reduce_sum | solution.py:60
  9.8 0.0 copy-done
  9.8 0.0 copy-done.15
  9.8 0.5 copy-done.2
  10.3 0.0 copy-start.14
  10.3 1.6 convolution_convert_fusion.1
  11.9 0.0 copy-done.14
  12.0 0.0 copy-start.12
  12.0 1.6 convolution_bitcast_fusion
  13.6 0.0 copy-start.16
  13.6 0.6 fusion.25
  14.2 0.0 copy-start.8
  14.2 0.0 copy-start.10
  14.2 0.7 pad_maximum_fusion
  14.9 4.0 %collective-permute-start.1 = (bf16[512,256]{0,1:T(8,128)(2,1)}, bf16[512,256]{0,1:T(8,128)(2,1)S(1)}, u32[]{:S(2)}, u32[]{:S(2)}) collective-permute-start(bf16[512,256]{0,1:T(8,128)(2,1)} %pad_maximum_fusion), channel_id=1, source_target_pairs={{0,8},{8,16},{16,24},{24,32},{32,40},{40,48},{48,56},{56,64},{64,7... | collective-permute-start | bytes 786440 | tf_op jit(solution)/shard_map/ppermute | solution.py:14
  18.9 5.6 %collective-permute-start = (bf16[512,256]{0,1:T(8,128)(2,1)}, bf16[512,256]{0,1:T(8,128)(2,1)}, u32[]{:S(2)}, u32[]{:S(2)}) collective-permute-start(bf16[512,256]{0,1:T(8,128)(2,1)} %pad_maximum_fusion), channel_id=1, source_target_pairs={{0,64},{8,72},{16,80},{24,88},{32,96},{40,104},{48,112},{56,120},{... | collective-permute-start | bytes 786440 | tf_op jit(solution)/shard_map/ppermute | solution.py:14
  24.5 0.0 copy-done.12
  24.5 0.0 copy-start.3
  24.5 0.1 dynamic_slice.7
  24.6 0.1 pad_dynamic-slice_fusion
  24.7 0.0 collective-permute-done.1
  24.7 0.0 copy-start.4
  24.7 0.1 maximum_maximum_fusion.1
  24.8 5.3 %collective-permute-start.2 = (bf16[1024,256]{0,1:T(8,128)(2,1)S(1)}, bf16[1024,256]{0,1:T(8,128)(2,1)S(1)}, u32[]{:S(2)}, u32[]{:S(2)}) collective-permute-start(bf16[1024,256]{0,1:T(8,128)(2,1)S(1)} %maximum_maximum_fusion.1), channel_id=1, source_target_pairs={{0,16},{8,24},{16,32},{24,40},{32,48},{40,56},{48,64},{56,72},{64,... | collective-permute-start | bytes 1572872 | tf_op jit(solution)/shard_map/ppermute | solution.py:14
  30.1 3.8 %fusion.5 = pred[512,4608]{0,1:T(8,128)(4,1)S(1)} fusion(s32[512]{0:T(512)S(1)} %dynamic_slice.7, s32[4608]{0:T(1024)S(1)} %get-tuple-element.16, s32[512]{0:T(512)S(1)} %iota_add_fusion.1, s32[4608]{0:T(1024)S(1)} %get-tuple-element.15), kind=kLoop, calls=%fused_computation.12 | loop fusion | flops 14155776 | bytes 2400256 | tf_op jit(solution)/shard_map/and | solution.py:92
  33.8 5.9 %collective-permute-done.2 = bf16[1024,256]{0,1:T(8,128)(2,1)S(1)} collective-permute-done((bf16[1024,256]{0,1:T(8,128)(2,1)S(1)}, bf16[1024,256]{0,1:T(8,128)(2,1)S(1)}, u32[]{:S(2)}, u32[]{:S(2)}) %collective-permute-start.2) | collective-permute-done | bytes 524320 | tf_op jit(solution)/shard_map/ppermute | solution.py:14
  39.7 0.0 copy-start.6
  39.7 1.1 maximum_maximum_fusion
  40.9 7.5 %collective-permute-start.3 = (bf16[2048,256]{0,1:T(8,128)(2,1)}, bf16[2048,256]{0,1:T(8,128)(2,1)}, u32[]{:S(2)}, u32[]{:S(2)}) collective-permute-start(bf16[2048,256]{0,1:T(8,128)(2,1)} %maximum_maximum_fusion), channel_id=1, source_target_pairs={{0,32},{8,40},{16,48},{24,56},{32,64},{40,72},{48,80},{56,88},{64,... | collective-permute-start | bytes 3145736 | tf_op jit(solution)/shard_map/ppermute | solution.py:14
  48.4 0.0 copy-done.16
  48.4 0.0 copy-done.3
  48.4 4.8 %fusion.30 = f32[512,512]{0,1:T(8,128)S(1)} fusion(bf16[4096,512]{1,0:T(8,128)(2,1)} %param.9, bf16[512,4096]{1,0:T(8,128)(2,1)S(1)} %copy-done.3, f32[4096]{0:T(1024)S(1)} %copy-done.16, f32[512]{0:T(512)S(1)} %add_rsqrt_fusion), kind=kOutput, calls=%fused_computation.59 | convolution fusion | flops 2155872256 | bytes 9455616 | tf_op jit(solution)/shard_map/dot_general | solution.py:31
  53.2 0.0 copy-done.8
  53.2 0.0 copy-done.10
  53.2 0.0 copy-done.4
  53.2 0.0 copy-done.6
  53.2 1.1 fusion.34
  54.3 1.4 copy.16
  55.6 2.4 %copy.15 = f32[512,4,64]{2,0,1:T(8,128)} copy(f32[512,4,64]{0,2,1:T(8,128)} %get-tuple-element.8) | data formatting | bytes 1048576
  58.0 0.0 copy-start.7
  58.0 1.0 multiply_cosine_fusion
  59.0 1.5 subtract_convert_fusion
  60.5 0.0 collective-permute-done
  60.6 1.0 constant_dynamic-update-slice_fusion.4
  61.5 5.6 %collective-permute-done.3 = bf16[2048,256]{0,1:T(8,128)(2,1)} collective-permute-done((bf16[2048,256]{0,1:T(8,128)(2,1)}, bf16[2048,256]{0,1:T(8,128)(2,1)}, u32[]{:S(2)}, u32[]{:S(2)}) %collective-permute-start.3) | collective-permute-done | bytes 1048608 | tf_op jit(solution)/shard_map/ppermute | solution.py:14
  67.1 1.3 constant_dynamic-update-slice_fusion.3
  68.5 0.0 copy-done.7
  68.5 0.0 copy-done.5
  68.5 0.0 copy-done.9
  68.6 0.0 copy-done.11
  68.6 0.0 copy-start.13
  68.6 15.3 %fusion.1 = (f32[4,512]{1,0:T(4,128)S(1)}, f32[4608,512,4]{1,0,2:T(8,128)}) fusion(pred[512,4608]{0,1:T(8,128)(4,1)S(1)} %fusion.5, bf16[512,4,64]{2,0,1:T(8,128)(2,1)S(1)} %get-tuple-element.6, bf16[512,4,64]{2,0,1:T(8,128)(2,1)S(1)} %get-tuple-element.5, bf16[4608,256]{0,1:T(8,128)(2,1)S(1)} %constant_dynamic-update-slice_fusion), kind=kOutput, calls=%fused_computation.4 | convolution fusion | flops 2445277184 | bytes 42344448 | tf_op jit(solution)/shard_map/tkgd,skd->kgts/dot_general | solution.py:40
  83.9 0.0 copy-done.13
  83.9 16.0 %fusion = f32[4,512]{1,0:T(4,128)S(1)} fusion(f32[4608,512,4]{1,0,2:T(8,128)} %get-tuple-element.14, f32[4,512]{1,0:T(4,128)S(1)} %get-tuple-element.13, pred[512,4608]{0,1:T(8,128)(4,1)S(1)} %fusion.5), kind=kLoop, calls=%fused_computation.3 | loop fusion | flops 37746688 | bytes 40124416 | tf_op jit(solution)/shard_map/reduce_sum | solution.py:46
  99.9 18.3 %fusion.9 = bf16[128,4,512]{2,0,1:T(8,128)(2,1)} fusion(f32[4,512]{1,0:T(4,128)S(1)} %fusion, f32[4,512]{1,0:T(4,128)S(1)} %get-tuple-element.13, f32[4608,512,4]{1,0,2:T(8,128)} %get-tuple-element.14, pred[512,4608]{0,1:T(8,128)(4,1)S(1)} %fusion.5, bf16[4608,256]{0,1:T(8,128)(2,1)} %copy-done.13), kind=kOutput, calls=%fused_computation.17 | convolution fusion | flops 2463367168 | bytes 41828352 | tf_op jit(solution)/shard_map/kgts,skd->tkgd/dot_general | solution.py:48
  118.2 0.0 all-gather.2.cloned.1.call-update
  118.3 0.0 copy-start.1
  118.3 48.9 %all-gather.2.cloned.1.call-done = bf16[512,4096]{0,1:T(8,128)(2,1)} async-done(((bf16[512,512]{0,1:T(8,128)(2,1)}), bf16[512,4096]{0,1:T(8,128)(2,1)}) %all-gather.2.cloned.1.call-update) | async-done | bytes 4194320 | tf_op jit(solution)/shard_map/all_gather | solution.py:96
  167.2 6.6 %convolution_convert_fusion = bf16[512,512]{1,0:T(8,128)(2,1)} fusion(bf16[512,4096]{0,1:T(8,128)(2,1)} %all-gather.2.cloned.1.call-done, bf16[4096,512]{1,0:T(8,128)(2,1)} %param.12), kind=kOutput, calls=%fused_computation.16 | convolution fusion | flops 2147745792 | bytes 8912896 | tf_op jit(solution)/shard_map/dot_general | solution.py:95
  173.8 0.0 copy-done.1
  (10 shorter events, 0.1 us)
Async XLA Ops:
  6.5 3.3 %copy-start = (bf16[4096,128]{1,0:T(8,128)(2,1)S(1)}, bf16[4096,128]{1,0:T(8,128)(2,1)}, u32[]{:S(2)}) copy-start(bf16[4096,128]{1,0:T(8,128)(2,1)} %param.11) | copy-start | bytes 3145732
  6.5 3.3 %copy-start.15 = (f32[4096]{0:T(1024)S(1)}, f32[4096]{0:T(1024)}, u32[]{:S(2)}) copy-start(f32[4096]{0:T(1024)} %param.8) | copy-start | bytes 49156
  6.5 160.7 %all-gather.2.cloned.1.call-start = ((), (), s32[]{:S(2)}) async-start(), calls=%async_computation | async-start | bytes 4718592 | tf_op jit(solution)/shard_map/all_gather | solution.py:96
  6.6 3.8 %copy-start.2 = (bf16[512,4096]{1,0:T(8,128)(2,1)S(1)}, bf16[512,4096]{1,0:T(8,128)(2,1)}, u32[]{:S(2)}) copy-start(bf16[512,4096]{1,0:T(8,128)(2,1)} %param.7) | copy-start | bytes 12582916
  10.3 1.6 copy-start.14
  12.0 12.6 %copy-start.12 = (s32[16384]{0:T(1024)S(1)}, s32[16384]{0:T(1024)}, u32[]{:S(2)}) copy-start(s32[16384]{0:T(1024)} %param.13) | copy-start | bytes 196612
  13.6 34.8 %copy-start.16 = (f32[4096]{0:T(1024)S(1)}, f32[4096]{0:T(1024)}, u32[]{:S(2)}) copy-start(f32[4096]{0:T(1024)} %param.8) | copy-start | bytes 49156
  14.2 39.0 %copy-start.8 = (bf16[512,64]{0,1:T(8,128)(2,1)}, bf16[512,64]{0,1:T(8,128)(2,1)S(1)}, u32[]{:S(2)}) copy-start(bf16[512,64]{0,1:T(8,128)(2,1)S(1)} %get-tuple-element.9) | copy-start | bytes 196612
  14.2 39.0 %copy-start.10 = (bf16[512,64]{0,1:T(8,128)(2,1)}, bf16[512,64]{0,1:T(8,128)(2,1)S(1)}, u32[]{:S(2)}) copy-start(bf16[512,64]{0,1:T(8,128)(2,1)S(1)} %get-tuple-element.10) | copy-start | bytes 196612
  14.9 9.8 %collective-permute-start.1 = (bf16[512,256]{0,1:T(8,128)(2,1)}, bf16[512,256]{0,1:T(8,128)(2,1)S(1)}, u32[]{:S(2)}, u32[]{:S(2)}) collective-permute-start(bf16[512,256]{0,1:T(8,128)(2,1)} %pad_maximum_fusion), channel_id=1, source_target_pairs={{0,8},{8,16},{16,24},{24,32},{32,40},{40,48},{48,56},{56,64},{64,7... | collective-permute-start | bytes 786440 | tf_op jit(solution)/shard_map/ppermute | solution.py:14
  18.9 41.6 %collective-permute-start = (bf16[512,256]{0,1:T(8,128)(2,1)}, bf16[512,256]{0,1:T(8,128)(2,1)}, u32[]{:S(2)}, u32[]{:S(2)}) collective-permute-start(bf16[512,256]{0,1:T(8,128)(2,1)} %pad_maximum_fusion), channel_id=1, source_target_pairs={{0,64},{8,72},{16,80},{24,88},{32,96},{40,104},{48,112},{56,120},{... | collective-permute-start | bytes 786440 | tf_op jit(solution)/shard_map/ppermute | solution.py:14
  24.5 23.9 %copy-start.3 = (bf16[512,4096]{1,0:T(8,128)(2,1)S(1)}, bf16[512,4096]{1,0:T(8,128)(2,1)}, u32[]{:S(2)}) copy-start(bf16[512,4096]{1,0:T(8,128)(2,1)} %param.7) | copy-start | bytes 12582916
  24.7 28.5 %copy-start.4 = (bf16[512,256]{0,1:T(8,128)(2,1)}, bf16[512,256]{0,1:T(8,128)(2,1)S(1)}, u32[]{:S(2)}) copy-start(bf16[512,256]{0,1:T(8,128)(2,1)S(1)} %collective-permute-done.1) | copy-start | bytes 786436
  24.8 15.0 %collective-permute-start.2 = (bf16[1024,256]{0,1:T(8,128)(2,1)S(1)}, bf16[1024,256]{0,1:T(8,128)(2,1)S(1)}, u32[]{:S(2)}, u32[]{:S(2)}) collective-permute-start(bf16[1024,256]{0,1:T(8,128)(2,1)S(1)} %maximum_maximum_fusion.1), channel_id=1, source_target_pairs={{0,16},{8,24},{16,32},{24,40},{32,48},{40,56},{48,64},{56,72},{64,... | collective-permute-start | bytes 1572872 | tf_op jit(solution)/shard_map/ppermute | solution.py:14
  39.7 13.5 %copy-start.6 = (bf16[1024,256]{0,1:T(8,128)(2,1)}, bf16[1024,256]{0,1:T(8,128)(2,1)S(1)}, u32[]{:S(2)}) copy-start(bf16[1024,256]{0,1:T(8,128)(2,1)S(1)} %collective-permute-done.2) | copy-start | bytes 1572868
  40.9 26.3 %collective-permute-start.3 = (bf16[2048,256]{0,1:T(8,128)(2,1)}, bf16[2048,256]{0,1:T(8,128)(2,1)}, u32[]{:S(2)}, u32[]{:S(2)}) collective-permute-start(bf16[2048,256]{0,1:T(8,128)(2,1)} %maximum_maximum_fusion), channel_id=1, source_target_pairs={{0,32},{8,40},{16,48},{24,56},{32,64},{40,72},{48,80},{56,88},{64,... | collective-permute-start | bytes 3145736 | tf_op jit(solution)/shard_map/ppermute | solution.py:14
  58.0 10.4 %copy-start.7 = (bf16[1024,256]{0,1:T(8,128)(2,1)S(1)}, bf16[1024,256]{0,1:T(8,128)(2,1)}, u32[]{:S(2)}) copy-start(bf16[1024,256]{0,1:T(8,128)(2,1)} %copy-done.6) | copy-start | bytes 1572868
  58.0 10.5 %copy-start.5 = (bf16[512,256]{0,1:T(8,128)(2,1)S(1)}, bf16[512,256]{0,1:T(8,128)(2,1)}, u32[]{:S(2)}) copy-start(bf16[512,256]{0,1:T(8,128)(2,1)} %copy-done.4) | copy-start | bytes 786436
  58.0 10.5 %copy-start.9 = (bf16[512,64]{0,1:T(8,128)(2,1)S(1)}, bf16[512,64]{0,1:T(8,128)(2,1)}, u32[]{:S(2)}) copy-start(bf16[512,64]{0,1:T(8,128)(2,1)} %copy-done.8) | copy-start | bytes 196612
  58.0 10.5 %copy-start.11 = (bf16[512,64]{0,1:T(8,128)(2,1)S(1)}, bf16[512,64]{0,1:T(8,128)(2,1)}, u32[]{:S(2)}) copy-start(bf16[512,64]{0,1:T(8,128)(2,1)} %copy-done.10) | copy-start | bytes 196612
  68.6 15.3 %copy-start.13 = (bf16[4608,256]{0,1:T(8,128)(2,1)}, bf16[4608,256]{0,1:T(8,128)(2,1)S(1)}, u32[]{:S(2)}) copy-start(bf16[4608,256]{0,1:T(8,128)(2,1)S(1)} %constant_dynamic-update-slice_fusion) | copy-start | bytes 7077892
  118.3 55.5 %copy-start.1 = (bf16[4096,128]{1,0:T(8,128)(2,1)S(1)}, bf16[4096,128]{1,0:T(8,128)(2,1)}, u32[]{:S(2)}) copy-start(bf16[4096,128]{1,0:T(8,128)(2,1)} %param.11) | copy-start | bytes 3145732
Sparse Core Ops, SparseCore 0:
  118.4 48.7 all-gather.1
where the time goes:
time: 181 us
  waiting for transfers between devices  60.5 us (33%)
  matrix products  48.2 us (27%)
  other arithmetic  28.1 us (16%)
  starting transfers between devices  22.4 us (12%)
  between operations  13.7 us (8%)
  local copies, waits for them, and re-layouts  7.74 us (4%)
    all_gather x1, waiting for transfers between devices, shards(): lax.all_gather(attended, 'tp', axis=1, tiled=True)  48.9 us
    ppermute x4, starting transfers between devices, shifted(): lax.ppermute(value, axis, [(source, source + steps) for source in range(l...  22.4 us
    dot_general x1, matrix products, attend(): jnp.einsum('kgts,skd->tkgd', probabilities, values, preferred_element_typ...  18.3 us
    reduce_sum x1, other arithmetic, attend(): totals = jnp.sum(weights, axis=-1, keepdims=True)  16 us
    dot_general x1, matrix products, attend(): jnp.einsum('tkgd,skd->kgts', grouped, keys, preferred_element_type=jnp.fl...  15.3 us
    ppermute x4, waiting for transfers between devices, shifted(): lax.ppermute(value, axis, [(source, source + steps) for source in range(l...  11.6 us
    unnamed x40, local copies, waits for them, and re-layouts  6.61 us
    dot_general x1, matrix products, shards(): jnp.dot(lax.all_gather(attended, 'tp', axis=1, tiled=True), out_weight, p...  6.61 us
  transfers between devices with their start and end apart: 5, of which 3 were waited for; matrix products, arithmetic and copies ran while one was open for 10% of the time, Pallas kernels for 0%

commit v1 on v0

--- a/solution.py
+++ b/solution.py
@@ -6,6 +6,11 @@
 
 HEAD_DIM = 128
 WINDOW = 4096
+
+
+def gather_by_exchange(array, axis, dim):
+    copies = jnp.concatenate([array] * lax.axis_size(axis), axis=dim)
+    return lax.all_to_all(copies, axis, dim, dim, tiled=True)
 
 
 def shifted(value, axis, steps):
@@ -93,9 +98,7 @@
     )
     attended = attend(queries, window_keys, window_values, allowed)
     projected = jnp.dot(
-        lax.all_gather(attended, "tp", axis=1, tiled=True),
-        out_weight,
-        preferred_element_type=jnp.float32,
+        gather_by_exchange(attended, "tp", 1), out_weight, preferred_element_type=jnp.float32
     )
     return projected.astype(jnp.bfloat16)
 

time: 181 us -> 191 us (1.055)
  the two profiles are of different devices: /device:TPU:1 before, /device:TPU:136 now
where the time goes in v1:
time: 191 us; the launch traced here: 190 us
  blocking collectives  53.9 us (28%)
  matrix products  47.7 us (25%)
  waiting for transfers between devices  32.5 us (17%)
  other arithmetic  28.2 us (15%)
  local copies, waits for them, and re-layouts  14.9 us (8%)
  starting transfers between devices  13 us (7%)
    all_to_all x1, blocking collectives, gather_by_exchange(): return lax.all_to_all(copies, axis, dim, dim, tiled=True)  53.9 us
    ppermute x4, waiting for transfers between devices, shifted(): lax.ppermute(value, axis, [(source, source + steps) for source in range(l...  32.5 us
    dot_general x1, matrix products, attend(): jnp.einsum('kgts,skd->tkgd', probabilities, values, preferred_element_typ...  17.6 us
    reduce_sum x1, other arithmetic, attend(): totals = jnp.sum(weights, axis=-1, keepdims=True)  16 us
    dot_general x1, matrix products, attend(): jnp.einsum('tkgd,skd->kgts', grouped, keys, preferred_element_type=jnp.fl...  15.3 us
    ppermute x4, starting transfers between devices, shifted(): lax.ppermute(value, axis, [(source, source + steps) for source in range(l...  13 us
    dot_general x1, matrix products, shards(): jnp.dot(gather_by_exchange(attended, 'tp', 1), out_weight, preferred_elem...  6.68 us
    unnamed x40, local copies, waits for them, and re-layouts  6.61 us
  transfers between devices with their start and end apart: 4, of which 3 were waited for; matrix products, arithmetic and copies ran while one was open for 10% of the time, Pallas kernels for 0%

profile of v1, /device:TPU:136, one launch (start us, length us, event | category | flops | bytes accessed | tf_op | source)
XLA Modules:
  0.0 190.5 jit_solution(8420284735642032241)
XLA Ops:
  0.0 0.0 copy-start
  0.0 0.0 copy-start.15
  0.0 0.0 copy-start.2
  0.0 3.2 %fusion.6 = f32[512]{0:T(512)S(1)} fusion(bf16[512,4096]{1,0:T(8,128)(2,1)} %param.7), kind=kLoop, calls=%fused_computation.13 | loop fusion | flops 6290944 | bytes 4196352 | tf_op jit(solution)/shard_map/reduce_sum | solution.py:65
  3.3 0.0 copy-done
  3.3 0.0 copy-done.15
  3.3 0.5 copy-done.2
  3.8 0.0 copy-start.14
  3.8 1.6 convolution_convert_fusion.1
  5.4 0.0 copy-done.14
  5.4 0.0 copy-start.12
  5.4 1.6 convolution_bitcast_fusion
  7.0 0.0 copy-start.16
  7.1 0.6 fusion.25
  7.6 0.0 copy-start.8
  7.6 0.0 copy-start.10
  7.6 0.7 pad_maximum_fusion
  8.4 3.5 %collective-permute-start.1 = (bf16[512,256]{0,1:T(8,128)(2,1)}, bf16[512,256]{0,1:T(8,128)(2,1)S(1)}, u32[]{:S(2)}, u32[]{:S(2)}) collective-permute-start(bf16[512,256]{0,1:T(8,128)(2,1)} %pad_maximum_fusion), channel_id=1, source_target_pairs={{0,8},{8,16},{16,24},{24,32},{32,40},{40,48},{48,56},{56,64},{64,7... | collective-permute-start | bytes 786440 | tf_op jit(solution)/shard_map/ppermute | solution.py:19
  11.9 3.4 %collective-permute-start = (bf16[512,256]{0,1:T(8,128)(2,1)}, bf16[512,256]{0,1:T(8,128)(2,1)}, u32[]{:S(2)}, u32[]{:S(2)}) collective-permute-start(bf16[512,256]{0,1:T(8,128)(2,1)} %pad_maximum_fusion), channel_id=1, source_target_pairs={{0,64},{8,72},{16,80},{24,88},{32,96},{40,104},{48,112},{56,120},{... | collective-permute-start | bytes 786440 | tf_op jit(solution)/shard_map/ppermute | solution.py:19
  15.2 0.0 copy-done.12
  15.3 0.0 copy-start.3
  15.3 0.1 dynamic_slice.7
  15.3 0.1 pad_dynamic-slice_fusion
  15.4 3.1 %collective-permute-done.1 = bf16[512,256]{0,1:T(8,128)(2,1)S(1)} collective-permute-done((bf16[512,256]{0,1:T(8,128)(2,1)}, bf16[512,256]{0,1:T(8,128)(2,1)S(1)}, u32[]{:S(2)}, u32[]{:S(2)}) %collective-permute-start.1) | collective-permute-done | bytes 262176 | tf_op jit(solution)/shard_map/ppermute | solution.py:19
  18.5 0.0 copy-start.4
  18.5 0.1 maximum_maximum_fusion.1
  18.6 4.2 %collective-permute-start.2 = (bf16[1024,256]{0,1:T(8,128)(2,1)S(1)}, bf16[1024,256]{0,1:T(8,128)(2,1)S(1)}, u32[]{:S(2)}, u32[]{:S(2)}) collective-permute-start(bf16[1024,256]{0,1:T(8,128)(2,1)S(1)} %maximum_maximum_fusion.1), channel_id=1, source_target_pairs={{0,16},{8,24},{16,32},{24,40},{32,48},{40,56},{48,64},{56,72},{64,... | collective-permute-start | bytes 1572872 | tf_op jit(solution)/shard_map/ppermute | solution.py:19
  22.8 3.8 %fusion.5 = pred[512,4608]{0,1:T(8,128)(4,1)S(1)} fusion(s32[512]{0:T(512)S(1)} %dynamic_slice.7, s32[4608]{0:T(1024)S(1)} %get-tuple-element.16, s32[512]{0:T(512)S(1)} %iota_add_fusion.1, s32[4608]{0:T(1024)S(1)} %get-tuple-element.15), kind=kLoop, calls=%fused_computation.12 | loop fusion | flops 14155776 | bytes 2400256 | tf_op jit(solution)/shard_map/and | solution.py:97
  26.5 17.1 %collective-permute-done.2 = bf16[1024,256]{0,1:T(8,128)(2,1)S(1)} collective-permute-done((bf16[1024,256]{0,1:T(8,128)(2,1)S(1)}, bf16[1024,256]{0,1:T(8,128)(2,1)S(1)}, u32[]{:S(2)}, u32[]{:S(2)}) %collective-permute-start.2) | collective-permute-done | bytes 524320 | tf_op jit(solution)/shard_map/ppermute | solution.py:19
  43.6 0.0 copy-start.6
  43.6 1.2 maximum_maximum_fusion
  44.8 1.9 %collective-permute-start.3 = (bf16[2048,256]{0,1:T(8,128)(2,1)}, bf16[2048,256]{0,1:T(8,128)(2,1)}, u32[]{:S(2)}, u32[]{:S(2)}) collective-permute-start(bf16[2048,256]{0,1:T(8,128)(2,1)} %maximum_maximum_fusion), channel_id=1, source_target_pairs={{0,32},{8,40},{16,48},{24,56},{32,64},{40,72},{48,80},{56,88},{64,... | collective-permute-start | bytes 3145736 | tf_op jit(solution)/shard_map/ppermute | solution.py:19
  46.7 0.0 copy-done.16
  46.7 0.0 copy-done.3
  46.7 4.8 %fusion.30 = f32[512,512]{0,1:T(8,128)S(1)} fusion(bf16[4096,512]{1,0:T(8,128)(2,1)} %param.9, bf16[512,4096]{1,0:T(8,128)(2,1)S(1)} %copy-done.3, f32[4096]{0:T(1024)S(1)} %copy-done.16, f32[512]{0:T(512)S(1)} %add_rsqrt_fusion), kind=kOutput, calls=%fused_computation.59 | convolution fusion | flops 2155872256 | bytes 9455616 | tf_op jit(solution)/shard_map/dot_general | solution.py:36
  51.5 0.0 copy-done.8
  51.5 0.0 copy-done.10
  51.5 0.0 copy-done.4
  51.6 0.0 copy-done.6
  51.6 1.1 fusion.34
  52.6 1.4 copy.28
  54.0 2.4 %copy.27 = f32[512,4,64]{2,0,1:T(8,128)} copy(f32[512,4,64]{0,2,1:T(8,128)} %get-tuple-element.8) | data formatting | bytes 1048576
  56.4 0.0 copy-start.7
  56.4 1.0 multiply_cosine_fusion
  57.4 1.5 subtract_convert_fusion
  58.9 0.0 collective-permute-done
  58.9 1.0 constant_dynamic-update-slice_fusion.4
  59.9 12.4 %collective-permute-done.3 = bf16[2048,256]{0,1:T(8,128)(2,1)} collective-permute-done((bf16[2048,256]{0,1:T(8,128)(2,1)}, bf16[2048,256]{0,1:T(8,128)(2,1)}, u32[]{:S(2)}, u32[]{:S(2)}) %collective-permute-start.3) | collective-permute-done | bytes 1048608 | tf_op jit(solution)/shard_map/ppermute | solution.py:19
  72.3 1.3 constant_dynamic-update-slice_fusion.3
  73.6 0.0 copy-done.7
  73.6 0.0 copy-done.5
  73.7 0.0 copy-done.9
  73.7 0.0 copy-done.11
  73.7 0.0 copy-start.13
  73.7 15.3 %fusion.1 = (f32[4,512]{1,0:T(4,128)S(1)}, f32[4608,512,4]{1,0,2:T(8,128)}) fusion(pred[512,4608]{0,1:T(8,128)(4,1)S(1)} %fusion.5, bf16[512,4,64]{2,0,1:T(8,128)(2,1)S(1)} %get-tuple-element.6, bf16[512,4,64]{2,0,1:T(8,128)(2,1)S(1)} %get-tuple-element.5, bf16[4608,256]{0,1:T(8,128)(2,1)S(1)} %constant_dynamic-update-slice_fusion), kind=kOutput, calls=%fused_computation.4 | convolution fusion | flops 2445277184 | bytes 42344448 | tf_op jit(solution)/shard_map/tkgd,skd->kgts/dot_general | solution.py:45
  89.1 0.0 copy-done.13
  89.1 16.0 %fusion = f32[4,512]{1,0:T(4,128)S(1)} fusion(f32[4608,512,4]{1,0,2:T(8,128)} %get-tuple-element.14, f32[4,512]{1,0:T(4,128)S(1)} %get-tuple-element.13, pred[512,4608]{0,1:T(8,128)(4,1)S(1)} %fusion.5), kind=kLoop, calls=%fused_computation.3 | loop fusion | flops 37746688 | bytes 40124416 | tf_op jit(solution)/shard_map/reduce_sum | solution.py:51
  105.1 17.6 %fusion.9 = bf16[128,4,512]{2,0,1:T(8,128)(2,1)S(1)} fusion(f32[4,512]{1,0:T(4,128)S(1)} %fusion, f32[4,512]{1,0:T(4,128)S(1)} %get-tuple-element.13, f32[4608,512,4]{1,0,2:T(8,128)} %get-tuple-element.14, pred[512,4608]{0,1:T(8,128)(4,1)S(1)} %fusion.5, bf16[4608,256]{0,1:T(8,128)(2,1)} %copy-done.13), kind=kOutput, calls=%fused_computation.17 | convolution fusion | flops 2463367168 | bytes 41828352 | tf_op jit(solution)/shard_map/kgts,skd->tkgd/dot_general | solution.py:53
  122.7 0.2 copy.22
  122.9 0.4 concatenate.48
  123.3 53.9 %all_to_all.9 = bf16[512,8,512]{2,0,1:T(8,128)(2,1)} all-to-all(bf16[512,8,512]{2,0,1:T(8,128)(2,1)S(1)} %concatenate.48), channel_id=1, replica_groups=mesh['seq'=32,'tp'=8] {'tp'}, dimensions={1} | all-to-all | bytes 8388608 | tf_op jit(solution)/shard_map/all_to_all | solution.py:13
  177.2 6.6 %copy.23 = bf16[512,8,512]{0,2,1:T(8,128)(2,1)} copy(bf16[512,8,512]{2,0,1:T(8,128)(2,1)} %all_to_all.9) | data formatting | bytes 8388608 | tf_op jit(solution)/shard_map/all_to_all | solution.py:13
  183.8 6.7 %convolution_convert_fusion = bf16[512,512]{1,0:T(8,128)(2,1)} fusion(bf16[512,4096]{0,1:T(8,128)(2,1)} %bitcast.46, bf16[4096,512]{1,0:T(8,128)(2,1)} %param.12), kind=kOutput, calls=%fused_computation.16 | convolution fusion | flops 2147745792 | bytes 8912896 | tf_op jit(solution)/shard_map/dot_general | solution.py:100
  190.5 0.0 copy-done.1
  (11 shorter events, 0.1 us)
Async XLA Ops:
  0.0 3.3 %copy-start = (bf16[4096,128]{1,0:T(8,128)(2,1)S(1)}, bf16[4096,128]{1,0:T(8,128)(2,1)}, u32[]{:S(2)}) copy-start(bf16[4096,128]{1,0:T(8,128)(2,1)} %param.11) | copy-start | bytes 3145732
  0.0 3.3 %copy-start.15 = (f32[4096]{0:T(1024)S(1)}, f32[4096]{0:T(1024)}, u32[]{:S(2)}) copy-start(f32[4096]{0:T(1024)} %param.8) | copy-start | bytes 49156
  0.0 3.8 %copy-start.2 = (bf16[512,4096]{1,0:T(8,128)(2,1)S(1)}, bf16[512,4096]{1,0:T(8,128)(2,1)}, u32[]{:S(2)}) copy-start(bf16[512,4096]{1,0:T(8,128)(2,1)} %param.7) | copy-start | bytes 12582916
  3.8 1.6 copy-start.14
  5.4 9.8 %copy-start.12 = (s32[16384]{0:T(1024)S(1)}, s32[16384]{0:T(1024)}, u32[]{:S(2)}) copy-start(s32[16384]{0:T(1024)} %param.13) | copy-start | bytes 196612
  7.0 39.7 %copy-start.16 = (f32[4096]{0:T(1024)S(1)}, f32[4096]{0:T(1024)}, u32[]{:S(2)}) copy-start(f32[4096]{0:T(1024)} %param.8) | copy-start | bytes 49156
  7.6 43.9 %copy-start.8 = (bf16[512,64]{0,1:T(8,128)(2,1)}, bf16[512,64]{0,1:T(8,128)(2,1)S(1)}, u32[]{:S(2)}) copy-start(bf16[512,64]{0,1:T(8,128)(2,1)S(1)} %get-tuple-element.9) | copy-start | bytes 196612
  7.6 43.9 %copy-start.10 = (bf16[512,64]{0,1:T(8,128)(2,1)}, bf16[512,64]{0,1:T(8,128)(2,1)S(1)}, u32[]{:S(2)}) copy-start(bf16[512,64]{0,1:T(8,128)(2,1)S(1)} %get-tuple-element.10) | copy-start | bytes 196612
  8.4 10.1 %collective-permute-start.1 = (bf16[512,256]{0,1:T(8,128)(2,1)}, bf16[512,256]{0,1:T(8,128)(2,1)S(1)}, u32[]{:S(2)}, u32[]{:S(2)}) collective-permute-start(bf16[512,256]{0,1:T(8,128)(2,1)} %pad_maximum_fusion), channel_id=1, source_target_pairs={{0,8},{8,16},{16,24},{24,32},{32,40},{40,48},{48,56},{56,64},{64,7... | collective-permute-start | bytes 786440 | tf_op jit(solution)/shard_map/ppermute | solution.py:19
  11.9 47.0 %collective-permute-start = (bf16[512,256]{0,1:T(8,128)(2,1)}, bf16[512,256]{0,1:T(8,128)(2,1)}, u32[]{:S(2)}, u32[]{:S(2)}) collective-permute-start(bf16[512,256]{0,1:T(8,128)(2,1)} %pad_maximum_fusion), channel_id=1, source_target_pairs={{0,64},{8,72},{16,80},{24,88},{32,96},{40,104},{48,112},{56,120},{... | collective-permute-start | bytes 786440 | tf_op jit(solution)/shard_map/ppermute | solution.py:19
  15.3 31.5 %copy-start.3 = (bf16[512,4096]{1,0:T(8,128)(2,1)S(1)}, bf16[512,4096]{1,0:T(8,128)(2,1)}, u32[]{:S(2)}) copy-start(bf16[512,4096]{1,0:T(8,128)(2,1)} %param.7) | copy-start | bytes 12582916
  18.5 33.0 %copy-start.4 = (bf16[512,256]{0,1:T(8,128)(2,1)}, bf16[512,256]{0,1:T(8,128)(2,1)S(1)}, u32[]{:S(2)}) copy-start(bf16[512,256]{0,1:T(8,128)(2,1)S(1)} %collective-permute-done.1) | copy-start | bytes 786436
  18.6 25.1 %collective-permute-start.2 = (bf16[1024,256]{0,1:T(8,128)(2,1)S(1)}, bf16[1024,256]{0,1:T(8,128)(2,1)S(1)}, u32[]{:S(2)}, u32[]{:S(2)}) collective-permute-start(bf16[1024,256]{0,1:T(8,128)(2,1)S(1)} %maximum_maximum_fusion.1), channel_id=1, source_target_pairs={{0,16},{8,24},{16,32},{24,40},{32,48},{40,56},{48,64},{56,72},{64,... | collective-permute-start | bytes 1572872 | tf_op jit(solution)/shard_map/ppermute | solution.py:19
  43.6 7.9 %copy-start.6 = (bf16[1024,256]{0,1:T(8,128)(2,1)}, bf16[1024,256]{0,1:T(8,128)(2,1)S(1)}, u32[]{:S(2)}) copy-start(bf16[1024,256]{0,1:T(8,128)(2,1)S(1)} %collective-permute-done.2) | copy-start | bytes 1572868
  44.8 27.5 %collective-permute-start.3 = (bf16[2048,256]{0,1:T(8,128)(2,1)}, bf16[2048,256]{0,1:T(8,128)(2,1)}, u32[]{:S(2)}, u32[]{:S(2)}) collective-permute-start(bf16[2048,256]{0,1:T(8,128)(2,1)} %maximum_maximum_fusion), channel_id=1, source_target_pairs={{0,32},{8,40},{16,48},{24,56},{32,64},{40,72},{48,80},{56,88},{64,... | collective-permute-start | bytes 3145736 | tf_op jit(solution)/shard_map/ppermute | solution.py:19
  56.4 17.2 %copy-start.7 = (bf16[1024,256]{0,1:T(8,128)(2,1)S(1)}, bf16[1024,256]{0,1:T(8,128)(2,1)}, u32[]{:S(2)}) copy-start(bf16[1024,256]{0,1:T(8,128)(2,1)} %copy-done.6) | copy-start | bytes 1572868
  56.4 17.3 %copy-start.5 = (bf16[512,256]{0,1:T(8,128)(2,1)S(1)}, bf16[512,256]{0,1:T(8,128)(2,1)}, u32[]{:S(2)}) copy-start(bf16[512,256]{0,1:T(8,128)(2,1)} %copy-done.4) | copy-start | bytes 786436
  56.4 17.3 %copy-start.9 = (bf16[512,64]{0,1:T(8,128)(2,1)S(1)}, bf16[512,64]{0,1:T(8,128)(2,1)}, u32[]{:S(2)}) copy-start(bf16[512,64]{0,1:T(8,128)(2,1)} %copy-done.8) | copy-start | bytes 196612
  56.4 17.3 %copy-start.11 = (bf16[512,64]{0,1:T(8,128)(2,1)S(1)}, bf16[512,64]{0,1:T(8,128)(2,1)}, u32[]{:S(2)}) copy-start(bf16[512,64]{0,1:T(8,128)(2,1)} %copy-done.10) | copy-start | bytes 196612
  73.7 15.4 %copy-start.13 = (bf16[4608,256]{0,1:T(8,128)(2,1)}, bf16[4608,256]{0,1:T(8,128)(2,1)S(1)}, u32[]{:S(2)}) copy-start(bf16[4608,256]{0,1:T(8,128)(2,1)S(1)} %constant_dynamic-update-slice_fusion) | copy-start | bytes 7077892
  183.8 6.7 %copy-start.1 = (bf16[4096,128]{1,0:T(8,128)(2,1)S(1)}, bf16[4096,128]{1,0:T(8,128)(2,1)}, u32[]{:S(2)}) copy-start(bf16[4096,128]{1,0:T(8,128)(2,1)} %param.11) | copy-start | bytes 3145732
